TPU v7x, 32 devices: a whole 2x2x4 slice. The times are simulated.
32 devices in a mesh: frames: 8 (over y, x, core), pos: 4 (over z).
Axes of the slice: x: 2, y: 2, z: 4, core: 2. Of those that a mesh axis runs over, the one named last changes fastest.
Arguments:
- frames_in: bfloat16 [512, 16, 1024], P(('frames', 'pos')), may hold values from -6 to 6
- frame_valid: int32 [512], P(('frames', 'pos')), may hold values 0 or 1
- last_position: int32 [512], P(('frames', 'pos')), may hold values from 0 to 15
- weight_qkv: bfloat16 [16, 1024, 3072], P('pos', 'frames'), may hold values from -0.1875 to 0.1875
- weight_out: bfloat16 [16, 1024, 1024], P('pos', 'frames'), may hold values from -0.5 to 0.5
- weight_ffn: bfloat16 [16, 1024, 5632], P('pos', 'frames'), may hold values from -0.1875 to 0.1875
- weight_down: bfloat16 [16, 2816, 1024], P('pos', 'frames'), may hold values from -0.109375 to 0.109375
- gain_attn: bfloat16 [16, 1024], P('pos', 'frames'), may hold values from 0.5 to 1.5
- gain_ffn: bfloat16 [16, 1024], P('pos', 'frames'), may hold values from 0.5 to 1.5
- grad_out: bfloat16 [512, 16, 1024], P(('frames', 'pos')), may hold values from -6 to 6
Outputs:
- output: bfloat16 [512, 16, 1024], P(('frames', 'pos'))
- grad_input: bfloat16 [512, 16, 1024], P(('frames', 'pos'))
- grad_qkv: float32 [16, 1024, 3072], P('pos', 'frames')
- grad_wout: float32 [16, 1024, 1024], P('pos', 'frames')
- grad_ffn: float32 [16, 1024, 5632], P('pos', 'frames')
- grad_down: float32 [16, 2816, 1024], P('pos', 'frames')
- grad_gain_attn: float32 [16, 1024], P('pos', 'frames')
- grad_gain_ffn: float32 [16, 1024], P('pos', 'frames')
All inputs are finite; a program needn't handle non-finite values. No bound on the sum of `frame_valid` on one device may be relied on, other than what follows from the above.
Results may differ from a plain program's by a relative error of at most 0.015.
Values may be sent and summed in bfloat16 or wider, within the bound.
No kernel may reach another device: no remote copies, remote signals or barrier semaphores. Data moves between devices by JAX's collectives and lax.ppermute only.
A program may use at most 384 MiB of HBM per device.

v0:
```python
import jax
import jax.numpy as jnp
from jax import lax
from jax.sharding import PartitionSpec as P

HEADS = 16
HEAD = 64
FF = 2816
EPSILON = 1e-06
NEGATIVE = -1e30


def rms_forward(values, gain_row):
    inverse = lax.rsqrt(jnp.mean(values * values, axis=-1, keepdims=True) + EPSILON)
    normed = values * inverse
    return (normed * gain_row[None], normed, inverse)


def rms_backward(upstream, normed, inverse, gain_row):
    scaled = upstream * gain_row[None]
    row_inner = jnp.mean(scaled * normed, axis=-1, keepdims=True)
    return (inverse * (scaled - normed * row_inner), jnp.sum(upstream * normed, axis=0))


def project(pattern, left_side, right_side):
    return jnp.einsum(pattern, left_side, right_side, preferred_element_type=jnp.float32)


def split_heads(qkv_frames):
    frames = qkv_frames.shape[0]
    length = qkv_frames.shape[1]
    pieces = qkv_frames.reshape(frames, length, 3, HEADS, HEAD)
    return (pieces[:, :, 0], pieces[:, :, 1], pieces[:, :, 2])


def masked_scores(query, key_part):
    raw_scores = project("fqhe,fkhe->fhqk", query, key_part) * HEAD ** (-0.5)
    length = raw_scores.shape[-1]
    allowed = lax.broadcasted_iota(jnp.int32, (length, length), 0) >= lax.broadcasted_iota(
        jnp.int32, (length, length), 1
    )
    return jnp.where(allowed, raw_scores, NEGATIVE)


def on_device(
    frames_in,
    frame_valid,
    last_position,
    weight_qkv,
    weight_out,
    weight_ffn,
    weight_down,
    gain_attn,
    gain_ffn,
    grad_out,
):
    scale = HEAD ** (-0.5)
    slot_index = lax.broadcasted_iota(jnp.int32, (frames_in.shape[0], frames_in.shape[1]), 1)
    live_mask = (frame_valid[:, None] > 0) & (slot_index <= last_position[:, None])
    pos_rows = lax.all_to_all(frames_in, "pos", split_axis=1, concat_axis=0, tiled=True)
    full_qkv, full_out, full_gain_a = (
        lax.all_gather(weight_qkv, "frames", axis=1, tiled=True),
        lax.all_gather(weight_out, "frames", axis=1, tiled=True),
        lax.all_gather(gain_attn, "frames", axis=1, tiled=True),
    )
    gain_one = full_gain_a.astype(jnp.float32)
    residual = pos_rows.astype(jnp.float32)
    scaled_one, normed_one, inverse_one = rms_forward(residual, gain_one)
    normed_one_low = scaled_one.astype(jnp.bfloat16)
    qkv_rows = project("rpd,pde->rpe", normed_one_low, full_qkv).astype(jnp.bfloat16)
    qkv_frames = lax.all_to_all(qkv_rows, "pos", split_axis=0, concat_axis=1, tiled=True)
    query, key_part, value_part = split_heads(qkv_frames)
    scores = masked_scores(query, key_part)
    row_top = jnp.max(scores, axis=-1, keepdims=True)
    exponent = jnp.exp(scores - row_top)
    row_total = jnp.sum(exponent, axis=-1, keepdims=True)
    log_total = row_top + jnp.log(row_total)
    attend_low = (exponent / row_total).astype(jnp.bfloat16)
    mixed_heads = project("fhqk,fkhe->fqhe", attend_low, value_part)
    mixed_low = mixed_heads.reshape(frames_in.shape).astype(jnp.bfloat16)
    mixed_rows = lax.all_to_all(mixed_low, "pos", split_axis=1, concat_axis=0, tiled=True)
    middle = residual + project("rpd,pde->rpe", mixed_rows, full_out)
    full_ffn, full_down, full_gain_f = (
        lax.all_gather(weight_ffn, "frames", axis=1, tiled=True),
        lax.all_gather(weight_down, "frames", axis=1, tiled=True),
        lax.all_gather(gain_ffn, "frames", axis=1, tiled=True),
    )
    gain_two = full_gain_f.astype(jnp.float32)
    scaled_two, normed_two, inverse_two = rms_forward(middle, gain_two)
    normed_two_low = scaled_two.astype(jnp.bfloat16)
    gate_up = project("rpd,pde->rpe", normed_two_low, full_ffn)
    gate = gate_up[..., :FF]
    upward = gate_up[..., FF:]
    gate_sig = jax.nn.sigmoid(gate)
    hidden = (gate * gate_sig * upward).astype(jnp.bfloat16)
    result = middle + project("rpf,pfd->rpd", hidden, full_down)
    result_frames = lax.all_to_all(
        result.astype(jnp.bfloat16), "pos", split_axis=0, concat_axis=1, tiled=True
    )
    output = jnp.where(live_mask[:, :, None], result_frames, jnp.zeros_like(result_frames))
    upstream = jnp.where(live_mask[:, :, None], grad_out, jnp.zeros_like(grad_out))
    upstream_rows = lax.all_to_all(upstream, "pos", split_axis=1, concat_axis=0, tiled=True)
    back_ffn, back_down = (
        lax.all_gather(weight_ffn, "frames", axis=1, tiled=True),
        lax.all_gather(weight_down, "frames", axis=1, tiled=True),
    )
    grad_hidden = project("rpd,pfd->rpf", upstream_rows, back_down)
    term_down = project("rpf,rpd->pfd", hidden, upstream_rows)
    grad_upward = grad_hidden * gate * gate_sig
    grad_gate = grad_hidden * upward * gate_sig * (1.0 + gate * (1.0 - gate_sig))
    grad_gate_up = jnp.concatenate([grad_gate, grad_upward], axis=-1).astype(jnp.bfloat16)
    grad_normed_two = project("rpe,pde->rpd", grad_gate_up, back_ffn)
    term_ffn = project("rpd,rpe->pde", normed_two_low, grad_gate_up)
    grad_middle_norm, term_gain_f = rms_backward(grad_normed_two, normed_two, inverse_two, gain_two)
    grad_middle = upstream_rows.astype(jnp.float32) + grad_middle_norm
    sum_ffn, sum_down, sum_gain_f = (
        lax.psum_scatter(
            term_ffn.astype(jnp.bfloat16), "frames", scatter_dimension=1, tiled=True
        ).astype(jnp.float32),
        lax.psum_scatter(
            term_down.astype(jnp.bfloat16), "frames", scatter_dimension=1, tiled=True
        ).astype(jnp.float32),
        lax.psum_scatter(
            term_gain_f.astype(jnp.bfloat16), "frames", scatter_dimension=1, tiled=True
        ).astype(jnp.float32),
    )
    back_qkv, back_out = (
        lax.all_gather(weight_qkv, "frames", axis=1, tiled=True),
        lax.all_gather(weight_out, "frames", axis=1, tiled=True),
    )
    grad_branch = grad_middle.astype(jnp.bfloat16)
    grad_mixed = project("rpe,pde->rpd", grad_branch, back_out).astype(jnp.bfloat16)
    term_out = project("rpd,rpe->pde", mixed_rows, grad_branch)
    grad_mixed_frames = lax.all_to_all(grad_mixed, "pos", split_axis=0, concat_axis=1, tiled=True)
    grad_heads = grad_mixed_frames.reshape(query.shape)
    again_scores = masked_scores(query, key_part)
    attend = jnp.exp(again_scores - log_total)
    grad_value = project("fhqk,fqhe->fkhe", attend.astype(jnp.bfloat16), grad_heads)
    grad_attend = project("fqhe,fkhe->fhqk", grad_heads, value_part)
    row_inner = jnp.sum(attend * grad_attend, axis=-1, keepdims=True)
    grad_scores = (attend * (grad_attend - row_inner)).astype(jnp.bfloat16)
    grad_query = project("fhqk,fkhe->fqhe", grad_scores, key_part) * scale
    grad_key = project("fhqk,fqhe->fkhe", grad_scores, query) * scale
    grad_qkv_frames = (
        jnp.stack([grad_query, grad_key, grad_value], axis=2)
        .reshape(qkv_frames.shape)
        .astype(jnp.bfloat16)
    )
    grad_qkv_rows = lax.all_to_all(grad_qkv_frames, "pos", split_axis=1, concat_axis=0, tiled=True)
    grad_normed_one = project("rpe,pde->rpd", grad_qkv_rows, back_qkv)
    term_qkv = project("rpd,rpe->pde", normed_one_low, grad_qkv_rows)
    grad_input_norm, term_gain_a = rms_backward(grad_normed_one, normed_one, inverse_one, gain_one)
    grad_rows = (grad_middle + grad_input_norm).astype(jnp.bfloat16)
    grad_frames = lax.all_to_all(grad_rows, "pos", split_axis=0, concat_axis=1, tiled=True)
    sum_qkv, sum_out, sum_gain_a = (
        lax.psum_scatter(
            term_qkv.astype(jnp.bfloat16), "frames", scatter_dimension=1, tiled=True
        ).astype(jnp.float32),
        lax.psum_scatter(
            term_out.astype(jnp.bfloat16), "frames", scatter_dimension=1, tiled=True
        ).astype(jnp.float32),
        lax.psum_scatter(
            term_gain_a.astype(jnp.bfloat16), "frames", scatter_dimension=1, tiled=True
        ).astype(jnp.float32),
    )
    return (output, grad_frames, sum_qkv, sum_out, sum_ffn, sum_down, sum_gain_a, sum_gain_f)


def solution(mesh):
    placed = (
        P(("frames", "pos"), None, None),
        P(("frames", "pos")),
        P(("frames", "pos")),
        P("pos", "frames", None),
        P("pos", "frames", None),
        P("pos", "frames", None),
        P("pos", "frames", None),
        P("pos", "frames"),
        P("pos", "frames"),
        P(("frames", "pos"), None, None),
    )
    return jax.shard_map(
        on_device,
        mesh=mesh,
        in_specs=placed,
        out_specs=(
            P(("frames", "pos"), None, None),
            P(("frames", "pos"), None, None),
            P("pos", "frames", None),
            P("pos", "frames", None),
            P("pos", "frames", None),
            P("pos", "frames", None),
            P("pos", "frames"),
            P("pos", "frames"),
        ),
        check_vma=False,
    )
```

profile of v0, /device:TPU:0, one launch (start us, length us, event | category | flops | bytes accessed | tf_op | source)
XLA Modules:
  0.0 1377.5 jit_solution(14971009679618732410)
XLA Ops:
  17.4 8.9 all_gather.22
  32.6 105.4 %all-gather.5.cloned.1.call-done = bf16[4,1024,3072]{2,1,0:T(8,128)(2,1)} async-done(((bf16[4,128,3072]{2,1,0:T(8,128)(2,1)}), bf16[4,1024,3072]{2,1,0:T(8,128)(2,1)}) %all-gather.5.cloned.1.call-update) | async-done | bytes 25165840 | tf_op jit(solution)/shard_map/all_gather | solution.py:62
  138.0 12.6 fusion
  158.8 36.3 %all-to-all-done.1 = bf16[64,4,3072]{2,1,0:T(4,128)(2,1)} async-done(((bf16[64,4,3072]{2,1,0:T(4,128)(2,1)}), bf16[64,4,3072]{2,1,0:T(4,128)(2,1)}, u32[]{:S(2)}, u32[]{:S(2)}) %all-to-all-start.1) | async-done | bytes 1572896 | tf_op jit(solution)/shard_map/all_to_all | solution.py:71
  221.1 9.2 all_gather.25
  240.8 169.6 %all-gather.9.cloned.1.call-done = bf16[4,1024,5632]{2,1,0:T(8,128)(2,1)} async-done(((bf16[4,128,5632]{2,1,0:T(8,128)(2,1)}), bf16[4,1024,5632]{2,1,0:T(8,128)(2,1)}) %all-gather.9.cloned.1.call-update) | async-done | bytes 46137360 | tf_op jit(solution)/shard_map/all_gather | solution.py:84
  410.4 23.7 %convolution_bitcast_fusion = f32[64,4,5632]{2,0,1:T(8,128)} fusion(bf16[4,1024,5632]{2,1,0:T(8,128)(2,1)} %all-gather.9.cloned.1.call-done, f32[64,4,1024]{2,0,1:T(8,128)S(1)} %get-tuple-element.29, f32[4,1024]{1,0:T(4,128)S(1)} %convert_element_type.128, f32[64,4]{0,1:T(4,128)S(1)} %add_rsqrt_fusion.1), kind=kOutput, calls=%fused_computation.3 | convolution fusion | flops 2953576448 | bytes 52970496 | tf_op jit(solution)/shard_map/rpd,pde->rpe/dot_general | solution.py:26
  434.1 94.5 %all-gather.11.cloned.1.call-done = bf16[4,2816,1024]{2,1,0:T(8,128)(2,1)} async-done(((bf16[4,352,1024]{2,1,0:T(8,128)(2,1)}), bf16[4,2816,1024]{2,1,0:T(8,128)(2,1)}) %all-gather.11.cloned.1.call-update) | async-done | bytes 23068688 | tf_op jit(solution)/shard_map/all_gather | solution.py:85
  528.7 14.3 %multiply_convert_fusion.1 = (bf16[64,4,2816]{2,0,1:T(8,128)(2,1)}, bf16[64,4,2816]{2,0,1:T(8,128)(2,1)}, bf16[64,4,2816]{2,0,1:T(8,128)(2,1)S(1)}) fusion(f32[64,4,5632]{2,0,1:T(8,128)} %convolution_bitcast_fusion, bf16[64,4,1024]{2,0,1:T(8,128)(2,1)} %bitcast.141, bf16[4,2816,1024]{2,1,0:T(8,128)(2,1)} %all-gather.11.cloned.1.call-done), kind=kOutput, calls=%fused_computation.11 | convolution fusion | flops 1487929344 | bytes 33685504 | tf_op jit(solution)/shard_map/rpd,pfd->rpf/dot_general | solution.py:26
  542.9 21.8 %multiply_reduce_fusion.1 = (bf16[4,1024]{1,0:T(4,128)(2,1)}, f32[64,4]{0,1:T(4,128)}, f32[64,4,1024]{2,0,1:T(8,128)}) fusion(f32[64,4,1024]{2,0,1:T(8,128)S(1)} %get-tuple-element.29, f32[64,4]{0,1:T(4,128)} %copy-done.15, f32[4,1024]{1,0:T(4,128)S(1)} %convert_element_type.128, bf16[4,1024,5632]{2,1,0:T(8,128)(2,1)} %all-gather.9.cloned.1.call-done, ...), kind=kOutput, calls=%fused_computation.45 | convolution fusion | flops 2960125696 | bytes 51144704 | tf_op jit(solution)/shard_map/rpe,pde->rpd/dot_general | solution.py:26
  581.2 13.4 all-to-all-done.5
  621.5 34.9 %all-to-all-done.6 = bf16[16,16,3072]{2,0,1:T(8,128)(2,1)} async-done(((bf16[16,16,3072]{2,0,1:T(8,128)(2,1)}), bf16[16,16,3072]{2,0,1:T(8,128)(2,1)}, u32[]{:S(2)}, u32[]{:S(2)}) %all-to-all-start.6) | async-done | bytes 1572896 | tf_op jit(solution)/shard_map/all_to_all | solution.py:149
  659.1 14.5 %multiply_reduce_fusion.2 = (bf16[4,1024]{1,0:T(4,128)(2,1)}, f32[64,4]{0,1:T(4,128)}, f32[64,4,1024]{2,0,1:T(8,128)}) fusion(f32[64,4,1024]{2,0,1:T(8,128)S(1)} %bitcast_multiply_fusion, f32[4,1024]{1,0:T(4,128)} %copy-done.12, bf16[64,4,3072]{2,0,1:T(8,128)(2,1)} %bitcast.135, bf16[4,1024,3072]{2,1,0:T(8,128)(2,1)} %all-gather.5.cloned.1.call-done), kind=kOutput, calls=%fused_computation.46 | convolution fusion | flops 1611919104 | bytes 28861440 | tf_op jit(solution)/shard_map/rpe,pde->rpd/dot_general | solution.py:26
  675.4 7.2 convolution_convert_fusion.3
  682.7 12.0 convolution_convert_fusion.2
  694.8 13.3 convolution_convert_fusion.1
  708.8 24.2 %convolution_convert_fusion = bf16[4,1024,5632]{2,1,0:T(8,128)(2,1)} fusion(bf16[64,4,2816]{2,0,1:T(8,128)(2,1)} %get-tuple-element.21, bf16[64,4,2816]{2,0,1:T(8,128)(2,1)} %get-tuple-element.20, f32[64,4,1024]{2,0,1:T(8,128)S(1)} %get-tuple-element.29, f32[4,1024]{1,0:T(4,128)S(1)} %convert_element_type.128, f32[64,4]{0,1:T(4,128)S(1)} %copy-done.16), kind=kOutput, calls=%fused_computation | convolution fusion | flops 2982412288 | bytes 50086912 | tf_op jit(solution)/shard_map/rpd,rpe->pde/dot_general | solution.py:26
  733.0 12.4 fusion.11
  754.0 10.1 all-to-all-done.3
  771.9 9.7 all-to-all-done.7
  785.5 146.9 %reduce-scatter.17.cloned.1.call-done = bf16[4,352,1024]{2,1,0:T(8,128)(2,1)} async-done(((bf16[4,2816,1024]{2,1,0:T(8,128)(2,1)}), bf16[4,352,1024]{2,1,0:T(8,128)(2,1)}) %reduce-scatter.17.cloned.1.call-update) | async-done | bytes 2883600 | tf_op jit(solution)/shard_map/reduce_scatter | solution.py:120
  937.5 155.9 %reduce-scatter.11.cloned.1.call-done = bf16[4,128,3072]{2,1,0:T(8,128)(2,1)} async-done(((bf16[4,1024,3072]{2,1,0:T(8,128)(2,1)}), bf16[4,128,3072]{2,1,0:T(8,128)(2,1)}) %reduce-scatter.11.cloned.1.call-update) | async-done | bytes 3145744 | tf_op jit(solution)/shard_map/reduce_scatter | solution.py:156
  1098.8 262.9 %reduce-scatter.15.cloned.1.call-done = bf16[4,128,5632]{2,1,0:T(8,128)(2,1)} async-done(((bf16[4,1024,5632]{2,1,0:T(8,128)(2,1)}), bf16[4,128,5632]{2,1,0:T(8,128)(2,1)}) %reduce-scatter.15.cloned.1.call-update) | async-done | bytes 5767184 | tf_op jit(solution)/shard_map/reduce_scatter | solution.py:117
  1361.7 8.6 convert_element_type.145
  (153 shorter events, 140.0 us)
Async XLA Ops:
  7.2 130.8 %all-gather.5.cloned.1.call-start = ((), (), s32[]{:S(2)}) async-start(), calls=%async_computation.14 | async-start | bytes 28311552 | tf_op jit(solution)/shard_map/all_gather | solution.py:62
  7.9 227.6 %all-gather.7.cloned.1.call-start = ((), (), s32[]{:S(2)}) async-start(), calls=%async_computation.15 | async-start | bytes 9437184 | tf_op jit(solution)/shard_map/all_gather | solution.py:63
  8.7 401.7 %all-gather.9.cloned.1.call-start = ((), (), s32[]{:S(2)}) async-start(), calls=%async_computation.16 | async-start | bytes 51904512 | tf_op jit(solution)/shard_map/all_gather | solution.py:84
  9.4 519.3 %all-gather.11.cloned.1.call-start = ((), (), s32[]{:S(2)}) async-start(), calls=%async_computation.17 | async-start | bytes 25952256 | tf_op jit(solution)/shard_map/all_gather | solution.py:85
  11.1 20.8 %all-to-all-start = ((bf16[16,16,1024]{2,0,1:T(8,128)(2,1)}), bf16[16,16,1024]{2,0,1:T(8,128)(2,1)S(1)}, u32[]{:S(2)}, u32[]{:S(2)}) async-start(bf16[16,16,1024]{2,0,1:T(8,128)(2,1)} %copy.63), calls=%async_computation | async-start | bytes 1048576 | tf_op jit(solution)/shard_map/all_to_all | solution.py:60
  26.3 124.3 %copy-start.12 = (f32[4,1024]{1,0:T(4,128)}, f32[4,1024]{1,0:T(4,128)S(1)}, u32[]{:S(2)}) copy-start(f32[4,1024]{1,0:T(4,128)S(1)} %convert_element_type.120) | copy-start | bytes 49156
  32.3 105.7 %copy-start.21 = (f32[64,4]{0,1:T(4,128)}, f32[64,4]{0,1:T(4,128)S(1)}, u32[]{:S(2)}) copy-start(f32[64,4]{0,1:T(4,128)S(1)} %rsqrt.20) | copy-start | bytes 3076
  32.4 203.1 %copy-start.2 = (f32[16,4,4,1024]{3,0,1,2:T(8,128)}, f32[16,4,4,1024]{3,0,1,2:T(8,128)S(1)}, u32[]{:S(2)}) copy-start(f32[16,4,4,1024]{3,0,1,2:T(8,128)S(1)} %copy.64) | copy-start | bytes 3145732
  153.0 42.1 %all-to-all-start.1 = ((bf16[64,4,3072]{2,1,0:T(4,128)(2,1)}), bf16[64,4,3072]{2,1,0:T(4,128)(2,1)}, u32[]{:S(2)}, u32[]{:S(2)}) async-start(bf16[64,4,3072]{2,1,0:T(4,128)(2,1)} %copy.68), calls=%async_computation.1 | async-start | bytes 3145728 | tf_op jit(solution)/shard_map/all_to_all | solution.py:71
  157.7 50.1 %copy-start.22 = (pred[16,16]{0,1:T(8,128)(4,1)}, pred[16,16]{0,1:T(8,128)(4,1)S(1)}, u32[]{:S(2)}) copy-start(pred[16,16]{0,1:T(8,128)(4,1)S(1)} %fusion.21) | copy-start | bytes 772
  195.1 20.9 %all-to-all-start.4 = ((bf16[16,16,1024]{2,0,1:T(8,128)(2,1)}), bf16[16,16,1024]{2,0,1:T(8,128)(2,1)}, u32[]{:S(2)}, u32[]{:S(2)}) async-start(bf16[16,16,1024]{2,0,1:T(8,128)(2,1)} %copy_select_fusion), calls=%async_computation.4 | async-start | bytes 1048576 | tf_op jit(solution)/shard_map/all_to_all | solution.py:102
  216.0 18.7 %all-to-all-start.2 = ((bf16[16,16,1024]{2,0,1:T(8,128)(2,1)}), bf16[16,16,1024]{2,0,1:T(8,128)(2,1)S(1)}, u32[]{:S(2)}, u32[]{:S(2)}) async-start(bf16[16,16,1024]{2,0,1:T(8,128)(2,1)} %reshape.126), calls=%async_computation.2 | async-start | bytes 1048576 | tf_op jit(solution)/shard_map/all_to_all | solution.py:81
  240.8 193.3 %copy-start.15 = (f32[64,4]{0,1:T(4,128)}, f32[64,4]{0,1:T(4,128)S(1)}, u32[]{:S(2)}) copy-start(f32[64,4]{0,1:T(4,128)S(1)} %add_rsqrt_fusion.1) | copy-start | bytes 3076
  574.8 19.8 %all-to-all-start.5 = ((bf16[64,4,1024]{2,1,0:T(4,128)(2,1)}), bf16[64,4,1024]{2,1,0:T(4,128)(2,1)}, u32[]{:S(2)}, u32[]{:S(2)}) async-start(bf16[64,4,1024]{2,1,0:T(4,128)(2,1)} %copy.81), calls=%async_computation.5 | async-start | bytes 1048576 | tf_op jit(solution)/shard_map/all_to_all | solution.py:134
  615.4 41.0 %all-to-all-start.6 = ((bf16[16,16,3072]{2,0,1:T(8,128)(2,1)}), bf16[16,16,3072]{2,0,1:T(8,128)(2,1)}, u32[]{:S(2)}, u32[]{:S(2)}) async-start(bf16[16,16,3072]{2,0,1:T(8,128)(2,1)} %reshape.127), calls=%async_computation.6 | async-start | bytes 3145728 | tf_op jit(solution)/shard_map/all_to_all | solution.py:149
  619.8 147.8 %reduce-scatter.21.cloned.1.call-start = ((), (), s32[]{:S(2)}) async-start(), calls=%async_computation.23 | async-start | bytes 294912
  621.4 149.0 %reduce-scatter.19.cloned.1.call-start = ((), (), s32[]{:S(2)}) async-start(), calls=%async_computation.22 | async-start | bytes 294912
  675.2 107.5 %reduce-scatter.13.cloned.1.call-start = ((), (), s32[]{:S(2)}) async-start(), calls=%async_computation.19 | async-start | bytes 9437184 | tf_op jit(solution)/shard_map/reduce_scatter | solution.py:159
  682.6 249.8 %reduce-scatter.17.cloned.1.call-start = ((), (), s32[]{:S(2)}) async-start(), calls=%async_computation.21 | async-start | bytes 25952256 | tf_op jit(solution)/shard_map/reduce_scatter | solution.py:120
  694.7 398.6 %reduce-scatter.11.cloned.1.call-start = ((), (), s32[]{:S(2)}) async-start(), calls=%async_computation.18 | async-start | bytes 28311552 | tf_op jit(solution)/shard_map/reduce_scatter | solution.py:156
  708.1 653.6 %reduce-scatter.15.cloned.1.call-start = ((), (), s32[]{:S(2)}) async-start(), calls=%async_computation.20 | async-start | bytes 51904512 | tf_op jit(solution)/shard_map/reduce_scatter | solution.py:117
  746.6 17.5 %all-to-all-start.3 = ((bf16[64,4,1024]{2,1,0:T(4,128)(2,1)}), bf16[64,4,1024]{2,1,0:T(4,128)(2,1)S(1)}, u32[]{:S(2)}, u32[]{:S(2)}) async-start(bf16[64,4,1024]{2,1,0:T(4,128)(2,1)} %copy.77), calls=%async_computation.3 | async-start | bytes 1048576 | tf_op jit(solution)/shard_map/all_to_all | solution.py:97
  750.8 18.4 %copy-start.23 = (pred[16,16]{0,1:T(8,128)(4,1)S(1)}, pred[16,16]{0,1:T(8,128)(4,1)}, u32[]{:S(2)}) copy-start(pred[16,16]{0,1:T(8,128)(4,1)} %copy-done.22) | copy-start | bytes 772
  764.1 17.4 %all-to-all-start.7 = ((bf16[64,4,1024]{2,1,0:T(4,128)(2,1)}), bf16[64,4,1024]{2,1,0:T(4,128)(2,1)S(1)}, u32[]{:S(2)}, u32[]{:S(2)}) async-start(bf16[64,4,1024]{2,1,0:T(4,128)(2,1)} %copy.89), calls=%async_computation.7 | async-start | bytes 1048576 | tf_op jit(solution)/shard_map/all_to_all | solution.py:154
  (22 other events, 106.7 us)
Sparse Core Ops, SparseCore 0:
  9.9 128.0 all-gather.4
  139.9 54.3 all-gather.6
  196.2 214.1 all-gather.8
  412.2 116.4 all-gather.10
  623.3 34.0 reduce-scatter.20
  675.3 31.7 reduce-scatter.18
  711.1 71.2 reduce-scatter.12
  786.5 145.8 reduce-scatter.16
  936.5 156.8 reduce-scatter.10
  1097.3 264.3 reduce-scatter.14
where the time goes:
time: 1380 us
  waiting for transfers between devices  1050 us (76%)
  matrix products  177 us (13%)
  local copies, waits for them, and re-layouts  46.6 us (3%)
  starting transfers between devices  37.2 us (3%)
  other arithmetic  33.2 us (2%)
  blocking collectives  18.1 us (1%)
  between operations  15.1 us (1%)
    reduce_scatter x1, waiting for transfers between devices, on_device(): lax.psum_scatter(term_ffn.astype(jnp.bfloat16), 'frames', scatter_dimensi...  263 us
    dot_general x18, matrix products, project(): jnp.einsum(pattern, left_side, right_side, preferred_element_type=jnp.flo...  177 us
    all_gather x1, waiting for transfers between devices, on_device(): lax.all_gather(weight_ffn, 'frames', axis=1, tiled=True)  170 us
    reduce_scatter x1, waiting for transfers between devices, on_device(): lax.psum_scatter(term_qkv.astype(jnp.bfloat16), 'frames', scatter_dimensi...  156 us
    reduce_scatter x1, waiting for transfers between devices, on_device(): lax.psum_scatter(term_down.astype(jnp.bfloat16), 'frames', scatter_dimens...  147 us
    all_gather x1, waiting for transfers between devices, on_device(): lax.all_gather(weight_qkv, 'frames', axis=1, tiled=True)  105 us
    all_gather x1, waiting for transfers between devices, on_device(): lax.all_gather(weight_down, 'frames', axis=1, tiled=True)  94.5 us
    all_to_all x1, waiting for transfers between devices, on_device(): lax.all_to_all(qkv_rows, 'pos', split_axis=0, concat_axis=1, tiled=True)  36.3 us
  transfers between devices with their start and end apart: 18, of which 13 were waited for; matrix products, arithmetic and copies ran while one was open for 13% of the time, Pallas kernels for 0%

commit v1 on v0

--- a/solution.py
+++ b/solution.py
@@ -54,6 +54,23 @@
     gain_ffn,
     grad_out,
 ):
+
+    def load_row(work_x):
+        width = lax.axis_size("frames")
+        by_rank = []
+        for dd in range(width):
+            by_rank.append((dd, (dd + 1) % width))
+        leaves = []
+        for dd in range(width):
+            leaves.append((dd, (dd - 1) % width))
+        met_up, latest = ([work_x], [work_x])
+        for _ in range(width // 2):
+            met_up.append(lax.ppermute(met_up[-1], "frames", by_rank))
+        for _ in range((width - 1) // 2):
+            latest.append(lax.ppermute(latest[-1], "frames", leaves))
+        view_out = jnp.concatenate([*met_up[::-1], *latest[1:]], axis=1)
+        return jnp.roll(view_out, (lax.axis_index("frames") - width // 2) * work_x.shape[1], axis=1)
+
     scale = HEAD ** (-0.5)
     slot_index = lax.broadcasted_iota(jnp.int32, (frames_in.shape[0], frames_in.shape[1]), 1)
     live_mask = (frame_valid[:, None] > 0) & (slot_index <= last_position[:, None])
@@ -82,7 +99,7 @@
     middle = residual + project("rpd,pde->rpe", mixed_rows, full_out)
     full_ffn, full_down, full_gain_f = (
         lax.all_gather(weight_ffn, "frames", axis=1, tiled=True),
-        lax.all_gather(weight_down, "frames", axis=1, tiled=True),
+        load_row(weight_down),
         lax.all_gather(gain_ffn, "frames", axis=1, tiled=True),
     )
     gain_two = full_gain_f.astype(jnp.float32)

time: 1380 us -> 1490 us (1.080)
  local copies, waits for them, and re-layouts: 46.6 us -> 98.2 us
  waiting for transfers between devices: 1050 us -> 1090 us
    ppermute x0 -> x7, waiting for transfers between devices: none -> 340 us  [the longest x4 332 us: load_row(): met_up.append(lax.ppermute(met_up[-1], 'frames', by_rank))]
    reduce_scatter x1, waiting for transfers between devices: 147 us -> 0.01 us  [on_device(): lax.psum_scatter(term_down.astype(jnp.bfloat16), 'frames', scatter_dimens...]
    reduce_scatter x1, waiting for transfers between devices: 156 us -> 11.6 us  [on_device(): lax.psum_scatter(term_qkv.astype(jnp.bfloat16), 'frames', scatter_dimensi...]
    unnamed x63 -> x90, local copies, waits for them, and re-layouts: 8.73 us -> 56.6 us
  transfers between devices with their start and end apart: 18 -> 25, of which waited for: 13 -> 18; matrix products, arithmetic and copies ran while one was open for 13% -> 15% of each run, Pallas kernels for 0% -> 0%
where the time goes in v1:
time: 1490 us; the launch traced here: 1480 us
  waiting for transfers between devices  1090 us (73%)
  matrix products  179 us (12%)
  local copies, waits for them, and re-layouts  98.2 us (7%)
  starting transfers between devices  46 us (3%)
  other arithmetic  33.2 us (2%)
  blocking collectives  18.3 us (1%)
  between operations  14.9 us (1%)
    ppermute x4, waiting for transfers between devices, load_row(): met_up.append(lax.ppermute(met_up[-1], 'frames', by_rank))  332 us
    reduce_scatter x1, waiting for transfers between devices, on_device(): lax.psum_scatter(term_ffn.astype(jnp.bfloat16), 'frames', scatter_dimensi...  263 us
    dot_general x18, matrix products, project(): jnp.einsum(pattern, left_side, right_side, preferred_element_type=jnp.flo...  179 us
    all_gather x1, waiting for transfers between devices, on_device(): lax.all_gather(weight_ffn, 'frames', axis=1, tiled=True)  169 us
    all_gather x1, waiting for transfers between devices, on_device(): lax.all_gather(weight_qkv, 'frames', axis=1, tiled=True)  105 us
    all_gather x1, waiting for transfers between devices, on_device(): lax.all_gather(weight_down, 'frames', axis=1, tiled=True)  94.5 us
    unnamed x90, local copies, waits for them, and re-layouts  56.6 us
    all_to_all x1, waiting for transfers between devices, on_device(): lax.all_to_all(qkv_rows, 'pos', split_axis=0, concat_axis=1, tiled=True)  36.3 us
  transfers between devices with their start and end apart: 25, of which 18 were waited for; matrix products, arithmetic and copies ran while one was open for 15% of the time, Pallas kernels for 0%

profile of v1, /device:TPU:0, one launch (start us, length us, event | category | flops | bytes accessed | tf_op | source)
XLA Modules:
  0.0 1481.5 jit_solution(7764616758972777838)
XLA Ops:
  17.4 8.9 all_gather.21
  32.6 105.4 %all-gather.5.cloned.1.call-done = bf16[4,1024,3072]{2,1,0:T(8,128)(2,1)} async-done(((bf16[4,128,3072]{2,1,0:T(8,128)(2,1)}), bf16[4,1024,3072]{2,1,0:T(8,128)(2,1)}) %all-gather.5.cloned.1.call-update) | async-done | bytes 25165840 | tf_op jit(solution)/shard_map/all_gather | solution.py:79
  138.0 12.6 fusion.2
  158.8 36.3 %all-to-all-done.1 = bf16[64,4,3072]{2,1,0:T(4,128)(2,1)} async-done(((bf16[64,4,3072]{2,1,0:T(4,128)(2,1)}), bf16[64,4,3072]{2,1,0:T(4,128)(2,1)}, u32[]{:S(2)}, u32[]{:S(2)}) %all-to-all-start.1) | async-done | bytes 1572896 | tf_op jit(solution)/shard_map/all_to_all | solution.py:88
  221.2 9.4 all_gather.24
  241.0 169.4 %all-gather.9.cloned.1.call-done = bf16[4,1024,5632]{2,1,0:T(8,128)(2,1)} async-done(((bf16[4,128,5632]{2,1,0:T(8,128)(2,1)}), bf16[4,1024,5632]{2,1,0:T(8,128)(2,1)}) %all-gather.9.cloned.1.call-update) | async-done | bytes 46137360 | tf_op jit(solution)/shard_map/all_gather | solution.py:101
  410.4 23.7 %convolution_bitcast_fusion = f32[64,4,5632]{2,0,1:T(8,128)} fusion(bf16[4,1024,5632]{2,1,0:T(8,128)(2,1)} %all-gather.9.cloned.1.call-done, f32[64,4,1024]{2,0,1:T(8,128)S(1)} %get-tuple-element.29, f32[4,1024]{1,0:T(4,128)S(1)} %convert_element_type.128, f32[64,4]{0,1:T(4,128)S(1)} %add_rsqrt_fusion.1), kind=kOutput, calls=%fused_computation.5 | convolution fusion | flops 2953576448 | bytes 52970496 | tf_op jit(solution)/shard_map/rpd,pde->rpe/dot_general | solution.py:26
  434.1 94.5 %all-gather.11.cloned.1.call-done = bf16[4,2816,1024]{2,1,0:T(8,128)(2,1)} async-done(((bf16[4,352,1024]{2,1,0:T(8,128)(2,1)}), bf16[4,2816,1024]{2,1,0:T(8,128)(2,1)}) %all-gather.11.cloned.1.call-update) | async-done | bytes 23068688 | tf_op jit(solution)/shard_map/all_gather | solution.py:122
  528.7 14.2 multiply_convert_fusion.1
  542.9 21.8 %multiply_reduce_fusion.1 = (bf16[4,1024]{1,0:T(4,128)(2,1)}, f32[64,4]{0,1:T(4,128)}, f32[64,4,1024]{2,0,1:T(8,128)}) fusion(f32[64,4,1024]{2,0,1:T(8,128)S(1)} %get-tuple-element.29, f32[64,4]{0,1:T(4,128)} %copy-done.21, f32[4,1024]{1,0:T(4,128)S(1)} %convert_element_type.128, bf16[4,1024,5632]{2,1,0:T(8,128)(2,1)} %all-gather.9.cloned.1.call-done, ...), kind=kOutput, calls=%fused_computation.45 | convolution fusion | flops 2960125696 | bytes 51144704 | tf_op jit(solution)/shard_map/rpe,pde->rpd/dot_general | solution.py:26
  581.1 13.4 all-to-all-done.5
  621.5 34.9 %all-to-all-done.6 = bf16[16,16,3072]{2,0,1:T(8,128)(2,1)} async-done(((bf16[16,16,3072]{2,0,1:T(8,128)(2,1)}), bf16[16,16,3072]{2,0,1:T(8,128)(2,1)}, u32[]{:S(2)}, u32[]{:S(2)}) %all-to-all-start.6) | async-done | bytes 1572896 | tf_op jit(solution)/shard_map/all_to_all | solution.py:166
  659.1 14.5 multiply_reduce_fusion.2
  682.7 11.9 convolution_convert_fusion.2
  694.8 13.3 convolution_convert_fusion.1
  708.7 24.2 %convolution_convert_fusion = bf16[4,1024,5632]{2,1,0:T(8,128)(2,1)} fusion(bf16[64,4,2816]{2,0,1:T(8,128)(2,1)} %get-tuple-element.21, bf16[64,4,2816]{2,0,1:T(8,128)(2,1)} %get-tuple-element.20, f32[64,4,1024]{2,0,1:T(8,128)S(1)} %get-tuple-element.29, f32[4,1024]{1,0:T(4,128)S(1)} %convert_element_type.128, f32[64,4]{0,1:T(4,128)S(1)} %copy-done.22), kind=kOutput, calls=%fused_computation | convolution fusion | flops 2982412288 | bytes 50086912 | tf_op jit(solution)/shard_map/rpd,rpe->pde/dot_general | solution.py:26
  733.0 68.7 %collective-permute-done = bf16[4,352,1024]{2,1,0:T(8,128)(2,1)S(1)} collective-permute-done((bf16[4,352,1024]{2,1,0:T(8,128)(2,1)}, bf16[4,352,1024]{2,1,0:T(8,128)(2,1)S(1)}, u32[]{:S(2)}, u32[]{:S(2)}) %collective-permute-start) | collective-permute-done | bytes 2883616 | tf_op jit(solution)/shard_map/ppermute | solution.py:68
  805.9 84.7 %collective-permute-done.1 = bf16[4,352,1024]{2,1,0:T(8,128)(2,1)S(1)} collective-permute-done((bf16[4,352,1024]{2,1,0:T(8,128)(2,1)S(1)}, bf16[4,352,1024]{2,1,0:T(8,128)(2,1)S(1)}, u32[]{:S(2)}, u32[]{:S(2)}) %collective-permute-start.1) | collective-permute-done | bytes 2883616 | tf_op jit(solution)/shard_map/ppermute | solution.py:68
  897.7 109.6 %collective-permute-done.2 = bf16[4,352,1024]{2,1,0:T(8,128)(2,1)} collective-permute-done((bf16[4,352,1024]{2,1,0:T(8,128)(2,1)S(1)}, bf16[4,352,1024]{2,1,0:T(8,128)(2,1)}, u32[]{:S(2)}, u32[]{:S(2)}) %collective-permute-start.2) | collective-permute-done | bytes 2883616 | tf_op jit(solution)/shard_map/ppermute | solution.py:68
  1015.5 69.4 %collective-permute-done.3 = bf16[4,352,1024]{2,1,0:T(8,128)(2,1)} collective-permute-done((bf16[4,352,1024]{2,1,0:T(8,128)(2,1)}, bf16[4,352,1024]{2,1,0:T(8,128)(2,1)}, u32[]{:S(2)}, u32[]{:S(2)}) %collective-permute-start.3) | collective-permute-done | bytes 2883616 | tf_op jit(solution)/shard_map/ppermute | solution.py:68
  1133.3 14.6 add_convert_fusion.1
  1186.1 11.6 reduce-scatter.11.cloned.1.call-done
  1203.1 262.8 %reduce-scatter.15.cloned.1.call-done = bf16[4,128,5632]{2,1,0:T(8,128)(2,1)} async-done(((bf16[4,1024,5632]{2,1,0:T(8,128)(2,1)}), bf16[4,128,5632]{2,1,0:T(8,128)(2,1)}) %reduce-scatter.15.cloned.1.call-update) | async-done | bytes 5767184 | tf_op jit(solution)/shard_map/reduce_scatter | solution.py:134
  1465.9 8.6 convert_element_type.145
  (195 shorter events, 228.2 us)
Async XLA Ops:
  7.2 130.8 %all-gather.5.cloned.1.call-start = ((), (), s32[]{:S(2)}) async-start(), calls=%async_computation.14 | async-start | bytes 28311552 | tf_op jit(solution)/shard_map/all_gather | solution.py:79
  7.9 227.9 %all-gather.7.cloned.1.call-start = ((), (), s32[]{:S(2)}) async-start(), calls=%async_computation.15 | async-start | bytes 9437184 | tf_op jit(solution)/shard_map/all_gather | solution.py:80
  8.7 401.7 %all-gather.9.cloned.1.call-start = ((), (), s32[]{:S(2)}) async-start(), calls=%async_computation.16 | async-start | bytes 51904512 | tf_op jit(solution)/shard_map/all_gather | solution.py:101
  9.4 519.2 %all-gather.11.cloned.1.call-start = ((), (), s32[]{:S(2)}) async-start(), calls=%async_computation.17 | async-start | bytes 25952256 | tf_op jit(solution)/shard_map/all_gather | solution.py:122
  11.1 20.8 %all-to-all-start = ((bf16[16,16,1024]{2,0,1:T(8,128)(2,1)}), bf16[16,16,1024]{2,0,1:T(8,128)(2,1)S(1)}, u32[]{:S(2)}, u32[]{:S(2)}) async-start(bf16[16,16,1024]{2,0,1:T(8,128)(2,1)} %copy.63), calls=%async_computation | async-start | bytes 1048576 | tf_op jit(solution)/shard_map/all_to_all | solution.py:77
  153.0 42.1 %all-to-all-start.1 = ((bf16[64,4,3072]{2,1,0:T(4,128)(2,1)}), bf16[64,4,3072]{2,1,0:T(4,128)(2,1)}, u32[]{:S(2)}, u32[]{:S(2)}) async-start(bf16[64,4,3072]{2,1,0:T(4,128)(2,1)} %copy.68), calls=%async_computation.1 | async-start | bytes 3145728 | tf_op jit(solution)/shard_map/all_to_all | solution.py:88
  195.1 21.1 %all-to-all-start.4 = ((bf16[16,16,1024]{2,0,1:T(8,128)(2,1)}), bf16[16,16,1024]{2,0,1:T(8,128)(2,1)}, u32[]{:S(2)}, u32[]{:S(2)}) async-start(bf16[16,16,1024]{2,0,1:T(8,128)(2,1)} %copy_select_fusion), calls=%async_computation.4 | async-start | bytes 1048576 | tf_op jit(solution)/shard_map/all_to_all | solution.py:119
  216.2 18.7 %all-to-all-start.2 = ((bf16[16,16,1024]{2,0,1:T(8,128)(2,1)}), bf16[16,16,1024]{2,0,1:T(8,128)(2,1)S(1)}, u32[]{:S(2)}, u32[]{:S(2)}) async-start(bf16[16,16,1024]{2,0,1:T(8,128)(2,1)} %reshape.126), calls=%async_computation.2 | async-start | bytes 1048576 | tf_op jit(solution)/shard_map/all_to_all | solution.py:98
  574.7 19.8 %all-to-all-start.5 = ((bf16[64,4,1024]{2,1,0:T(4,128)(2,1)}), bf16[64,4,1024]{2,1,0:T(4,128)(2,1)}, u32[]{:S(2)}, u32[]{:S(2)}) async-start(bf16[64,4,1024]{2,1,0:T(4,128)(2,1)} %copy.81), calls=%async_computation.5 | async-start | bytes 1048576 | tf_op jit(solution)/shard_map/all_to_all | solution.py:151
  615.5 40.9 %all-to-all-start.6 = ((bf16[16,16,3072]{2,0,1:T(8,128)(2,1)}), bf16[16,16,3072]{2,0,1:T(8,128)(2,1)}, u32[]{:S(2)}, u32[]{:S(2)}) async-start(bf16[16,16,3072]{2,0,1:T(8,128)(2,1)} %reshape.127), calls=%async_computation.6 | async-start | bytes 3145728 | tf_op jit(solution)/shard_map/all_to_all | solution.py:166
  619.8 547.0 %reduce-scatter.21.cloned.1.call-start = ((), (), s32[]{:S(2)}) async-start(), calls=%async_computation.23 | async-start | bytes 294912
  621.5 548.1 %reduce-scatter.19.cloned.1.call-start = ((), (), s32[]{:S(2)}) async-start(), calls=%async_computation.22 | async-start | bytes 294912
  675.2 503.0 %reduce-scatter.13.cloned.1.call-start = ((), (), s32[]{:S(2)}) async-start(), calls=%async_computation.19 | async-start | bytes 9437184 | tf_op jit(solution)/shard_map/reduce_scatter | solution.py:176
  682.7 498.3 %reduce-scatter.17.cloned.1.call-start = ((), (), s32[]{:S(2)}) async-start(), calls=%async_computation.21 | async-start | bytes 25952256 | tf_op jit(solution)/shard_map/reduce_scatter | solution.py:137
  694.7 503.0 %reduce-scatter.11.cloned.1.call-start = ((), (), s32[]{:S(2)}) async-start(), calls=%async_computation.18 | async-start | bytes 28311552 | tf_op jit(solution)/shard_map/reduce_scatter | solution.py:173
  708.0 757.9 %reduce-scatter.15.cloned.1.call-start = ((), (), s32[]{:S(2)}) async-start(), calls=%async_computation.20 | async-start | bytes 51904512 | tf_op jit(solution)/shard_map/reduce_scatter | solution.py:134
  732.9 68.8 %collective-permute-start = (bf16[4,352,1024]{2,1,0:T(8,128)(2,1)}, bf16[4,352,1024]{2,1,0:T(8,128)(2,1)S(1)}, u32[]{:S(2)}, u32[]{:S(2)}) collective-permute-start(bf16[4,352,1024]{2,1,0:T(8,128)(2,1)} %param.16), channel_id=1, source_target_pairs={{0,4},{4,8},{8,12},{12,16},{16,20},{20,24},{24,28},{28,0},{1,5},{5... | collective-permute-start | bytes 8650760 | tf_op jit(solution)/shard_map/ppermute | solution.py:68
  803.2 87.4 %collective-permute-start.1 = (bf16[4,352,1024]{2,1,0:T(8,128)(2,1)S(1)}, bf16[4,352,1024]{2,1,0:T(8,128)(2,1)S(1)}, u32[]{:S(2)}, u32[]{:S(2)}) collective-permute-start(bf16[4,352,1024]{2,1,0:T(8,128)(2,1)S(1)} %collective-permute-done), channel_id=1, source_target_pairs={{0,4},{4,8},{8,12},{12,16},{16,20},{20,24},{24,28},{28,0},{1,5},{5... | collective-permute-start | bytes 8650760 | tf_op jit(solution)/shard_map/ppermute | solution.py:68
  803.2 90.2 %collective-permute-start.4 = (bf16[4,352,1024]{2,1,0:T(8,128)(2,1)}, bf16[4,352,1024]{2,1,0:T(8,128)(2,1)S(1)}, u32[]{:S(2)}, u32[]{:S(2)}) collective-permute-start(bf16[4,352,1024]{2,1,0:T(8,128)(2,1)} %param.16), channel_id=1, source_target_pairs={{0,28},{4,0},{8,4},{12,8},{16,12},{20,16},{24,20},{28,24},{1,29},{... | collective-permute-start | bytes 8650760 | tf_op jit(solution)/shard_map/ppermute | solution.py:70
  890.6 116.7 %collective-permute-start.2 = (bf16[4,352,1024]{2,1,0:T(8,128)(2,1)S(1)}, bf16[4,352,1024]{2,1,0:T(8,128)(2,1)}, u32[]{:S(2)}, u32[]{:S(2)}) collective-permute-start(bf16[4,352,1024]{2,1,0:T(8,128)(2,1)S(1)} %collective-permute-done.1), channel_id=1, source_target_pairs={{0,4},{4,8},{8,12},{12,16},{16,20},{20,24},{24,28},{28,0},{1,5},{5... | collective-permute-start | bytes 8650760 | tf_op jit(solution)/shard_map/ppermute | solution.py:68
  895.0 117.2 %collective-permute-start.5 = (bf16[4,352,1024]{2,1,0:T(8,128)(2,1)S(1)}, bf16[4,352,1024]{2,1,0:T(8,128)(2,1)}, u32[]{:S(2)}, u32[]{:S(2)}) collective-permute-start(bf16[4,352,1024]{2,1,0:T(8,128)(2,1)S(1)} %collective-permute-done.4), channel_id=1, source_target_pairs={{0,28},{4,0},{8,4},{12,8},{16,12},{20,16},{24,20},{28,24},{1,29},{... | collective-permute-start | bytes 8650760 | tf_op jit(solution)/shard_map/ppermute | solution.py:70
  1007.3 77.5 %collective-permute-start.3 = (bf16[4,352,1024]{2,1,0:T(8,128)(2,1)}, bf16[4,352,1024]{2,1,0:T(8,128)(2,1)}, u32[]{:S(2)}, u32[]{:S(2)}) collective-permute-start(bf16[4,352,1024]{2,1,0:T(8,128)(2,1)} %collective-permute-done.2), channel_id=1, source_target_pairs={{0,4},{4,8},{8,12},{12,16},{16,20},{20,24},{24,28},{28,0},{1,5},{5... | collective-permute-start | bytes 8650760 | tf_op jit(solution)/shard_map/ppermute | solution.py:68
  1012.2 94.9 %collective-permute-start.6 = (bf16[4,352,1024]{2,1,0:T(8,128)(2,1)}, bf16[4,352,1024]{2,1,0:T(8,128)(2,1)}, u32[]{:S(2)}, u32[]{:S(2)}) collective-permute-start(bf16[4,352,1024]{2,1,0:T(8,128)(2,1)} %collective-permute-done.5), channel_id=1, source_target_pairs={{0,28},{4,0},{8,4},{12,8},{16,12},{20,16},{24,20},{28,24},{1,29},{... | collective-permute-start | bytes 8650760 | tf_op jit(solution)/shard_map/ppermute | solution.py:70
  1149.2 14.0 all-to-all-start.3
  (35 other events, 964.9 us)
Sparse Core Ops, SparseCore 0:
  9.9 128.0 all-gather.4
  139.9 54.3 all-gather.6
  196.2 214.1 all-gather.8
  412.2 116.4 all-gather.10
  623.4 34.0 reduce-scatter.20
  675.4 31.7 reduce-scatter.18
  711.2 89.0 reduce-scatter.12
  804.3 232.2 reduce-scatter.16
  1040.7 156.9 reduce-scatter.10
  1201.6 264.2 reduce-scatter.14
